TPU v7x, 128 devices: a whole 4x4x4 slice. The times are simulated.
128 devices in a mesh: dom: 16 (over y, z), sub: 8 (over x, core).
Axes of the slice: x: 4, y: 4, z: 4, core: 2. Of those that a mesh axis runs over, the one named last changes fastest.
Arguments:
- features: bfloat16 [131072, 256], P(('dom', 'sub')), may hold values from -6 to 6
- cotangent: bfloat16 [131072, 256], P(('dom', 'sub')), may hold values from -6 to 6
- w_self_one: bfloat16 [256, 256], replicated, may hold values from -0.375 to 0.375
- w_nbr_one: bfloat16 [256, 256], replicated, may hold values from -0.375 to 0.375
- bias_one: float32 [256], replicated, may hold values from -4 to 4
- w_self_two: bfloat16 [256, 256], replicated, may hold values from -0.375 to 0.375
- w_nbr_two: bfloat16 [256, 256], replicated, may hold values from -0.375 to 0.375
- in_count: int32 [131072], P(('dom', 'sub')), may hold values from 0 to 7
- send_list: int32 [128, 128, 4], P(('dom', 'sub')), may hold values from 0 to 1023
- src_slot: int32 [128, 2048], P(('dom', 'sub')), may hold values from 0 to 1535
- dst_slot: int32 [128, 2048], P(('dom', 'sub')), may hold values from 0 to 1535
- edge_count: int32 [128], P(('dom', 'sub')), may hold values from 512 to 2048, as said below
Outputs:
- grad_features: bfloat16 [131072, 256], P(('dom', 'sub'))
- grad_weights: float32 [4, 256, 256], replicated
- grad_bias: float32 [256], replicated
Inputs may be any that keep to these rules, and one draw needn't show every extreme that they name: Each device's first edge_count slots are live; one device has all 2048 live in every draw.
All inputs are finite; a program needn't handle non-finite values.
Results may differ from a plain program's by a relative error of at most 0.0056.
Values may be sent and summed in bfloat16 or wider, within the bound.
A program may use at most 64 MiB of HBM per device.

v0:
```python
import math
import jax
import jax.numpy as jnp
from jax import lax
from jax.sharding import PartitionSpec as P


def to_mirrors(master_rows, send_list):
    picked_rows = jnp.take(master_rows, send_list[0], axis=0)
    feature_dim = master_rows.shape[1]
    received = lax.all_to_all(picked_rows, ("dom", "sub"), split_axis=0, concat_axis=0, tiled=True)
    return received.reshape(-1, feature_dim)


def to_masters(mirror_partial, send_list, node_dev):
    feature_dim = mirror_partial.shape[1]
    per_peer = send_list.shape[2]
    sectioned_rows = mirror_partial.reshape(-1, per_peer, feature_dim)
    received = lax.all_to_all(
        sectioned_rows, ("dom", "sub"), split_axis=0, concat_axis=0, tiled=True
    )
    flat_rows = received.reshape(-1, feature_dim)
    owners = send_list[0].reshape(-1)
    placing = (jnp.arange(node_dev, dtype=jnp.int32)[:, None] == owners[None, :]).astype(
        jnp.float32
    )
    return jnp.dot(
        placing, flat_rows, precision=lax.Precision.HIGHEST, preferred_element_type=jnp.float32
    )


def spread(slot_table, from_slot, into_slot, live_count):
    slot_total = slot_table.shape[0]
    edge_slots = from_slot.shape[0]
    feature_dim = slot_table.shape[1]
    block_rows = math.gcd(512, edge_slots)
    slot_ids = jnp.arange(slot_total, dtype=jnp.int32)[None, :]

    def one_block(turn_index, total):
        offset = turn_index * block_rows
        from_part = lax.dynamic_slice_in_dim(from_slot, offset, block_rows)
        into_part = lax.dynamic_slice_in_dim(into_slot, offset, block_rows)
        live_rows = (jnp.arange(block_rows, dtype=jnp.int32) + offset < live_count)[:, None]
        picking = ((from_part[:, None] == slot_ids) & live_rows).astype(slot_table.dtype)
        picked_rows = jnp.dot(picking, slot_table, preferred_element_type=jnp.float32).astype(
            slot_table.dtype
        )
        placing = (into_part[:, None] == slot_ids).astype(slot_table.dtype)
        return total + tdot(placing, picked_rows)

    start_total = jnp.zeros((slot_total, feature_dim), jnp.float32)
    block_count = edge_slots // block_rows
    return lax.fori_loop(0, block_count, one_block, start_total)


def tdot(left, right):
    return lax.dot_general(
        left, right, (((0,), (0,)), ((), ())), preferred_element_type=jnp.float32
    )


def dot_transposed(left, right):
    return lax.dot_general(
        left, right, (((1,), (1,)), ((), ())), preferred_element_type=jnp.float32
    )


def silu_grad(value):
    sigmoid_v = jax.nn.sigmoid(value)
    return sigmoid_v * (1.0 + value * (1.0 - sigmoid_v))


def shards(
    features,
    cotangent,
    w_self_one,
    w_nbr_one,
    bias_one,
    w_self_two,
    w_nbr_two,
    in_count,
    send_list,
    src_slot,
    dst_slot,
    edge_count,
):
    node_dev = features.shape[0]
    sources = src_slot[0]
    targets = dst_slot[0]
    live_count = edge_count[0]
    inverse = (1.0 / jnp.maximum(in_count, 1).astype(jnp.float32))[:, None]

    def gather_sum(master_rows, from_slot, into_slot):
        slot_table = jnp.concatenate([master_rows, to_mirrors(master_rows, send_list)], axis=0)
        partial_value = spread(slot_table, from_slot, into_slot, live_count)
        return partial_value[:node_dev] + to_masters(partial_value[node_dev:], send_list, node_dev)

    mean_one = (gather_sum(features, sources, targets) * inverse).astype(jnp.bfloat16)
    z_one = (
        jnp.dot(features, w_self_one, preferred_element_type=jnp.float32)
        + jnp.dot(mean_one, w_nbr_one, preferred_element_type=jnp.float32)
        + bias_one
    )
    h_one = jax.nn.silu(z_one).astype(jnp.bfloat16)
    message_two = (dot_transposed(cotangent, w_nbr_two) * inverse).astype(jnp.bfloat16)
    forward_sum = gather_sum(h_one, sources, targets)
    backward_sum = gather_sum(message_two, targets, sources)
    mean_two = (forward_sum * inverse).astype(jnp.bfloat16)
    late_self = tdot(h_one, cotangent)
    late_nbr = tdot(mean_two, cotangent)
    grad_h_one = dot_transposed(cotangent, w_self_two) + backward_sum
    grad_z_one = (grad_h_one * silu_grad(z_one)).astype(jnp.bfloat16)
    message_one = (dot_transposed(grad_z_one, w_nbr_one) * inverse).astype(jnp.bfloat16)
    early_self = tdot(features, grad_z_one)
    early_nbr = tdot(mean_one, grad_z_one)
    early_bias = jnp.sum(grad_z_one.astype(jnp.float32), axis=0)
    grad_features = (
        dot_transposed(grad_z_one, w_self_one) + gather_sum(message_one, targets, sources)
    ).astype(jnp.bfloat16)
    self_one, nbr_one, bias_sum, self_two, nbr_two = lax.psum(
        (early_self, early_nbr, early_bias, late_self, late_nbr), ("dom", "sub")
    )
    norm_factor = jnp.float32(node_dev * lax.axis_size("dom") * lax.axis_size("sub")) ** (-0.5)
    grad_weights = jnp.stack([self_one, nbr_one, self_two, nbr_two]) * norm_factor
    grad_bias = bias_sum * norm_factor
    return (grad_features, grad_weights, grad_bias)


def solution(mesh):
    return jax.shard_map(
        shards,
        mesh=mesh,
        in_specs=(
            P(("dom", "sub"), None),
            P(("dom", "sub"), None),
            P(),
            P(),
            P(),
            P(),
            P(),
            P(("dom", "sub")),
            P(("dom", "sub"), None, None),
            P(("dom", "sub"), None),
            P(("dom", "sub"), None),
            P(("dom", "sub")),
        ),
        out_specs=(P(("dom", "sub"), None), P(), P()),
        check_vma=False,
    )
```

profile of v0, /device:TPU:1, one launch (start us, length us, event | category | flops | bytes accessed | tf_op | source)
XLA Modules:
  0.0 453.2 jit_solution(3980596526978102994)
XLA Ops:
  9.5 1.2 fusion.75
  10.8 2.0 gather_fusion
  12.9 2.0 gather_fusion.1
  15.0 1.2 broadcast_select_fusion.2
  16.2 11.9 %all-to-all-start = ((bf16[128,4,256]{2,1,0:T(4,128)(2,1)}), bf16[128,4,256]{2,1,0:T(4,128)(2,1)}, u32[]{:S(2)}, u32[]{:S(2)}) async-start(bf16[128,4,256]{2,1,0:T(4,128)(2,1)} %get-tuple-element.741), calls=%async_computation | async-start | bytes 524288 | tf_op jit(solution)/shard_map/all_to_all | solution.py:11
  29.0 9.7 %all-to-all-done = bf16[128,4,256]{2,1,0:T(4,128)(2,1)} async-done(((bf16[128,4,256]{2,1,0:T(4,128)(2,1)}), bf16[128,4,256]{2,1,0:T(4,128)(2,1)}, u32[]{:S(2)}, u32[]{:S(2)}) %all-to-all-start) | async-done | bytes 262176 | tf_op jit(solution)/shard_map/all_to_all | solution.py:11
  38.7 4.6 %all-to-all-start.2 = ((bf16[128,4,256]{2,1,0:T(4,128)(2,1)}), bf16[128,4,256]{2,1,0:T(4,128)(2,1)S(1)}, u32[]{:S(2)}, u32[]{:S(2)}) async-start(bf16[128,4,256]{2,1,0:T(4,128)(2,1)} %get-tuple-element.740), calls=%async_computation.2 | async-start | bytes 524288 | tf_op jit(solution)/shard_map/all_to_all | solution.py:11
  43.3 1.7 reshape.78
  45.0 1.9 pad_maximum_fusion
  46.9 20.3 %while.60 = (s32[]{:T(128)}, f32[1536,256]{1,0:T(8,128)S(1)}, s32[2048]{0:T(1024)S(1)}, s32[2048]{0:T(1024)}, s32[]{:T(128)}, /*index=5*/bf16[1536,256]{1,0:T(8,...) while((s32[]{:T(128)}, f32[1536,256]{1,0:T(8,128)S(1)}, s32[2048]{0:T(1024)S(1)}, ...), condition=%wide.region_1.3_spmd.clone.clone, body=%wide.region_0.0_spmd.clone.clone.sunk | while | flops 808584192 | bytes 3945645 | solution.py:53
  48.4 3.6 fusion.125
  53.5 3.6 fusion.125
  58.6 3.6 fusion.125
  63.7 3.6 fusion.125
  67.3 1.2 reshape.79
  68.7 9.8 %all-to-all-start.1 = ((f32[128,4,256]{2,1,0:T(4,128)}), f32[128,4,256]{2,1,0:T(4,128)S(1)}, u32[]{:S(2)}, u32[]{:S(2)}) async-start(f32[128,4,256]{2,1,0:T(4,128)} %reshape.79), calls=%async_computation.1 | async-start | bytes 1048576 | tf_op jit(solution)/shard_map/all_to_all | solution.py:19
  78.6 22.6 %while.61 = (s32[]{:T(128)}, f32[1536,256]{1,0:T(8,128)}, s32[2048]{0:T(1024)}, s32[2048]{0:T(1024)S(1)}, s32[]{:T(128)}, /*index=5*/bf16[1536,256]{1,0:T(8,128)...) while((s32[]{:T(128)}, f32[1536,256]{1,0:T(8,128)}, s32[2048]{0:T(1024)}, ...), condition=%wide.region_3.5_spmd.clone.clone, body=%wide.region_2.4_spmd.clone.clone.sunk | while | flops 808584192 | bytes 3945645 | solution.py:53
  80.1 3.1 fusion.128
  84.7 4.5 fusion.128
  90.7 4.5 fusion.128
  96.7 4.5 fusion.128
  101.2 1.1 slice.27
  102.3 0.9 reshape.82
  103.2 9.8 %all-to-all-start.3 = ((f32[128,4,256]{2,1,0:T(4,128)}), f32[128,4,256]{2,1,0:T(4,128)S(1)}, u32[]{:S(2)}, u32[]{:S(2)}) async-start(f32[128,4,256]{2,1,0:T(4,128)} %reshape.82), calls=%async_computation.3 | async-start | bytes 1048576 | tf_op jit(solution)/shard_map/all_to_all | solution.py:19
  113.0 1.3 fusion.82
  114.5 3.3 fusion.66
  117.8 8.8 %all-to-all-done.3 = f32[128,4,256]{2,1,0:T(4,128)S(1)} async-done(((f32[128,4,256]{2,1,0:T(4,128)}), f32[128,4,256]{2,1,0:T(4,128)S(1)}, u32[]{:S(2)}, u32[]{:S(2)}) %all-to-all-start.3) | async-done | bytes 524320 | tf_op jit(solution)/shard_map/all_to_all | solution.py:19
  126.8 2.3 fusion.73
  129.2 1.3 multiply_convert_fusion
  130.6 1.1 convert_reduce_fusion
  132.1 1.0 convolution_bitcast_fusion.3
  133.1 1.9 gather_fusion.2
  135.1 2.0 gather_fusion.3
  137.2 1.9 broadcast_select_fusion
  139.1 4.6 %all-to-all-start.6 = ((bf16[128,4,256]{2,1,0:T(4,128)(2,1)}), bf16[128,4,256]{2,1,0:T(4,128)(2,1)S(1)}, u32[]{:S(2)}, u32[]{:S(2)}) async-start(bf16[128,4,256]{2,1,0:T(4,128)(2,1)} %get-tuple-element.738), calls=%async_computation.6 | async-start | bytes 524288 | tf_op jit(solution)/shard_map/all_to_all | solution.py:11
  143.7 1.1 convolution_bitcast_fusion.2
  144.8 67.1 %psum.39 = f32[256]{0:T(256)S(1)} all-reduce(f32[256]{0:T(256)S(1)} %copy-done.15), channel_id=1, replica_groups=mesh['dom'=16,'sub'=8] {'dom','sub'}, use_global_device_ids=true, to_apply=%region_13.15 | all-reduce | flops 256 | bytes 2048 | tf_op jit(solution)/shard_map/psum | solution.py:120
  212.5 4.7 %all-to-all-start.4 = ((bf16[128,4,256]{2,1,0:T(4,128)(2,1)}), bf16[128,4,256]{2,1,0:T(4,128)(2,1)S(1)}, u32[]{:S(2)}, u32[]{:S(2)}) async-start(bf16[128,4,256]{2,1,0:T(4,128)(2,1)} %get-tuple-element.739), calls=%async_computation.4 | async-start | bytes 524288 | tf_op jit(solution)/shard_map/all_to_all | solution.py:11
  217.2 0.9 pad_maximum_fusion.3
  218.2 21.7 %while.63 = (s32[]{:T(128)}, f32[1536,256]{1,0:T(8,128)}, s32[2048]{0:T(1024)S(1)}, s32[2048]{0:T(1024)S(1)}, s32[]{:T(128)}, /*index=5*/bf16[1536,256]{1,0:T(8,...) while((s32[]{:T(128)}, f32[1536,256]{1,0:T(8,128)}, s32[2048]{0:T(1024)S(1)}, ...), condition=%wide.region_10.12_spmd.clone.clone, body=%wide.region_9.11_spmd.clone.clone.sunk | while | flops 808584192 | bytes 3945645 | solution.py:53
  219.0 4.2 fusion.134
  224.0 4.7 %fusion.134 = f32[1536,256]{1,0:T(8,128)} fusion(f32[1536,256]{1,0:T(8,128)} %get-tuple-element.995, s32[512]{0:T(512)S(1)} %dynamic_slice.86, bf16[1536,256]{1,0:T(8,128)(2,1)} %get-tuple-element.1009, s32[512]{0:T(512)S(1)} %dynamic_slice.87, pred[512]{0:T(512)(128)(4,1)S(1)} %add_compare_fusion.11, pred[]{:T(512)S(6)} %compare.15), kind=kOutput, calls=%fused_computation.46.clone.1 | convolution fusion | flops 808583168 | bytes 3936769 | tf_op jit(solution)/shard_map/while/body/eval_jaxpr/dot_general | solution.py:57
  229.6 4.7 %fusion.134 = f32[1536,256]{1,0:T(8,128)} fusion(f32[1536,256]{1,0:T(8,128)} %get-tuple-element.995, s32[512]{0:T(512)S(1)} %dynamic_slice.86, bf16[1536,256]{1,0:T(8,128)(2,1)} %get-tuple-element.1009, s32[512]{0:T(512)S(1)} %dynamic_slice.87, pred[512]{0:T(512)(128)(4,1)S(1)} %add_compare_fusion.11, pred[]{:T(512)S(6)} %compare.15), kind=kOutput, calls=%fused_computation.46.clone.1 | convolution fusion | flops 808583168 | bytes 3936769 | tf_op jit(solution)/shard_map/while/body/eval_jaxpr/dot_general | solution.py:57
  235.1 4.7 %fusion.134 = f32[1536,256]{1,0:T(8,128)} fusion(f32[1536,256]{1,0:T(8,128)} %get-tuple-element.995, s32[512]{0:T(512)S(1)} %dynamic_slice.86, bf16[1536,256]{1,0:T(8,128)(2,1)} %get-tuple-element.1009, s32[512]{0:T(512)S(1)} %dynamic_slice.87, pred[512]{0:T(512)(128)(4,1)S(1)} %add_compare_fusion.11, pred[]{:T(512)S(6)} %compare.15), kind=kOutput, calls=%fused_computation.46.clone.1 | convolution fusion | flops 808583168 | bytes 3936769 | tf_op jit(solution)/shard_map/while/body/eval_jaxpr/dot_general | solution.py:57
  239.9 1.1 slice.31
  241.0 0.9 reshape.88
  241.9 9.8 %all-to-all-start.7 = ((f32[128,4,256]{2,1,0:T(4,128)}), f32[128,4,256]{2,1,0:T(4,128)S(1)}, u32[]{:S(2)}, u32[]{:S(2)}) async-start(f32[128,4,256]{2,1,0:T(4,128)} %reshape.88), calls=%async_computation.7 | async-start | bytes 1048576 | tf_op jit(solution)/shard_map/all_to_all | solution.py:19
  252.7 21.8 %while.62 = (s32[]{:T(128)}, f32[1536,256]{1,0:T(8,128)}, s32[2048]{0:T(1024)S(1)}, s32[2048]{0:T(1024)S(1)}, s32[]{:T(128)}, /*index=5*/bf16[1536,256]{1,0:T(8,...) while((s32[]{:T(128)}, f32[1536,256]{1,0:T(8,128)}, s32[2048]{0:T(1024)S(1)}, ...), condition=%wide.region_5.7_spmd.clone.clone, body=%wide.region_4.6_spmd.clone.clone.sunk | while | flops 808584192 | bytes 3945645 | solution.py:53
  253.5 4.3 fusion.131
  258.6 4.8 %fusion.131 = f32[1536,256]{1,0:T(8,128)} fusion(f32[1536,256]{1,0:T(8,128)} %get-tuple-element.965, s32[512]{0:T(512)S(1)} %dynamic_slice.84, bf16[1536,256]{1,0:T(8,128)(2,1)} %get-tuple-element.979, s32[512]{0:T(512)S(1)} %dynamic_slice.85, pred[512]{0:T(512)(128)(4,1)S(1)} %add_compare_fusion.10, pred[]{:T(512)S(6)} %compare.14), kind=kOutput, calls=%fused_computation.35.clone.1 | convolution fusion | flops 808583168 | bytes 3936769 | tf_op jit(solution)/shard_map/while/body/eval_jaxpr/dot_general | solution.py:57
  264.1 4.8 %fusion.131 = f32[1536,256]{1,0:T(8,128)} fusion(f32[1536,256]{1,0:T(8,128)} %get-tuple-element.965, s32[512]{0:T(512)S(1)} %dynamic_slice.84, bf16[1536,256]{1,0:T(8,128)(2,1)} %get-tuple-element.979, s32[512]{0:T(512)S(1)} %dynamic_slice.85, pred[512]{0:T(512)(128)(4,1)S(1)} %add_compare_fusion.10, pred[]{:T(512)S(6)} %compare.14), kind=kOutput, calls=%fused_computation.35.clone.1 | convolution fusion | flops 808583168 | bytes 3936769 | tf_op jit(solution)/shard_map/while/body/eval_jaxpr/dot_general | solution.py:57
  269.7 4.8 %fusion.131 = f32[1536,256]{1,0:T(8,128)} fusion(f32[1536,256]{1,0:T(8,128)} %get-tuple-element.965, s32[512]{0:T(512)S(1)} %dynamic_slice.84, bf16[1536,256]{1,0:T(8,128)(2,1)} %get-tuple-element.979, s32[512]{0:T(512)S(1)} %dynamic_slice.85, pred[512]{0:T(512)(128)(4,1)S(1)} %add_compare_fusion.10, pred[]{:T(512)S(6)} %compare.14), kind=kOutput, calls=%fused_computation.35.clone.1 | convolution fusion | flops 808583168 | bytes 3936769 | tf_op jit(solution)/shard_map/while/body/eval_jaxpr/dot_general | solution.py:57
  274.5 1.1 slice.29
  275.6 0.9 reshape.85
  276.5 9.8 %all-to-all-start.5 = ((f32[128,4,256]{2,1,0:T(4,128)}), f32[128,4,256]{2,1,0:T(4,128)S(1)}, u32[]{:S(2)}, u32[]{:S(2)}) async-start(f32[128,4,256]{2,1,0:T(4,128)} %reshape.85), calls=%async_computation.5 | async-start | bytes 1048576 | tf_op jit(solution)/shard_map/all_to_all | solution.py:19
  286.3 1.1 convolution_bitcast_fusion.1
  287.6 2.3 fusion.72
  289.9 1.1 convolution_bitcast_fusion
  291.0 8.9 %all-to-all-done.5 = f32[128,4,256]{2,1,0:T(4,128)S(1)} async-done(((f32[128,4,256]{2,1,0:T(4,128)}), f32[128,4,256]{2,1,0:T(4,128)S(1)}, u32[]{:S(2)}, u32[]{:S(2)}) %all-to-all-start.5) | async-done | bytes 524320 | tf_op jit(solution)/shard_map/all_to_all | solution.py:19
  300.1 2.3 fusion.69
  302.4 1.1 fusion.76
  303.5 140.2 %all-reduce.3.cloned.1.call-done = (f32[1,256,256]{1,2,0:T(8,128)}, f32[1,256,256]{1,2,0:T(8,128)}, f32[1,256,256]{1,2,0:T(8,128)}, f32[1,256,256]{1,2,0:T(8,128)}) async-done(((f32[1,256,256]{1,2,0:T(8,128)}, f32[1,256,256]{1,2,0:T(8,128)}, f32[1,256,256]{1,2,0:T(8,128)}, f32[1,256,256]{1,2,0:T(8,128)}), (f32[1,256,256]{1,2,0:T(8,128)}, f32[1,256,256]{1,2,0:T(8,128)}, f32[1,256,256]{1,2,0:T(8,128)}, ...) | async-done | bytes 1048592 | tf_op jit(solution)/shard_map/psum | solution.py:120
  443.8 1.3 maximum_multiply_fusion
  445.0 1.3 copy.35
  (118 shorter events, 25.2 us)
Async XLA Ops:
  7.2 2.4 copy-start
  10.8 2.0 copy-start.1
  14.8 13.4 %copy-start.12 = (s32[1,128,4]{1,2,0:T(4,128)S(1)}, s32[1,128,4]{1,2,0:T(4,128)}, u32[]{:S(2)}) copy-start(s32[1,128,4]{1,2,0:T(4,128)} %param.30) | copy-start | bytes 6148
  15.0 1.2 copy-start.10
  16.2 30.7 %copy-start.8 = (s32[1,2048]{1,0:T(1,128)S(1)}, s32[1,2048]{1,0:T(1,128)}, u32[]{:S(2)}) copy-start(s32[1,2048]{1,0:T(1,128)} %param.31) | copy-start | bytes 24580
  16.2 22.5 %all-to-all-start = ((bf16[128,4,256]{2,1,0:T(4,128)(2,1)}), bf16[128,4,256]{2,1,0:T(4,128)(2,1)}, u32[]{:S(2)}, u32[]{:S(2)}) async-start(bf16[128,4,256]{2,1,0:T(4,128)(2,1)} %get-tuple-element.741), calls=%async_computation | async-start | bytes 524288 | tf_op jit(solution)/shard_map/all_to_all | solution.py:11
  38.7 29.8 %all-to-all-start.2 = ((bf16[128,4,256]{2,1,0:T(4,128)(2,1)}), bf16[128,4,256]{2,1,0:T(4,128)(2,1)S(1)}, u32[]{:S(2)}, u32[]{:S(2)}) async-start(bf16[128,4,256]{2,1,0:T(4,128)(2,1)} %get-tuple-element.740), calls=%async_computation.2 | async-start | bytes 524288 | tf_op jit(solution)/shard_map/all_to_all | solution.py:11
  67.3 1.4 copy-start.2
  68.7 34.5 %all-to-all-start.1 = ((f32[128,4,256]{2,1,0:T(4,128)}), f32[128,4,256]{2,1,0:T(4,128)S(1)}, u32[]{:S(2)}, u32[]{:S(2)}) async-start(f32[128,4,256]{2,1,0:T(4,128)} %reshape.79), calls=%async_computation.1 | async-start | bytes 1048576 | tf_op jit(solution)/shard_map/all_to_all | solution.py:19
  101.2 11.8 %copy-start.7 = (bf16[256,256]{1,0:T(8,128)(2,1)S(1)}, bf16[256,256]{1,0:T(8,128)(2,1)}, u32[]{:S(2)}) copy-start(bf16[256,256]{1,0:T(8,128)(2,1)} %param.24) | copy-start | bytes 393220
  103.2 23.4 %all-to-all-start.3 = ((f32[128,4,256]{2,1,0:T(4,128)}), f32[128,4,256]{2,1,0:T(4,128)S(1)}, u32[]{:S(2)}, u32[]{:S(2)}) async-start(f32[128,4,256]{2,1,0:T(4,128)} %reshape.82), calls=%async_computation.3 | async-start | bytes 1048576 | tf_op jit(solution)/shard_map/all_to_all | solution.py:19
  113.0 1.5 copy-start.13
  117.8 11.3 %copy-start.4 = (f32[1024,256]{1,0:T(8,128)S(1)}, f32[1024,256]{1,0:T(8,128)}, u32[]{:S(2)}) copy-start(f32[1024,256]{1,0:T(8,128)} %fusion.82) | copy-start | bytes 3145732
  117.8 11.4 %copy-start.11 = (bf16[256,256]{1,0:T(8,128)(2,1)S(1)}, bf16[256,256]{1,0:T(8,128)(2,1)}, u32[]{:S(2)}) copy-start(bf16[256,256]{1,0:T(8,128)(2,1)} %param.25) | copy-start | bytes 393220
  129.2 1.3 copy-start.5
  129.2 1.4 copy-start.3
  129.2 1.4 copy-start.16
  137.1 6.6 %copy-start.6 = (bf16[1024,256]{1,0:T(8,128)(2,1)S(1)}, bf16[1024,256]{1,0:T(8,128)(2,1)}, u32[]{:S(2)}) copy-start(bf16[1024,256]{1,0:T(8,128)(2,1)} %copy-done.5) | copy-start | bytes 1572868
  137.2 7.6 %copy-start.15 = (f32[256]{0:T(256)S(1)}, f32[256]{0:T(256)}, u32[]{:S(2)}) copy-start(f32[256]{0:T(256)} %get-tuple-element.744) | copy-start | bytes 3076
  139.1 73.4 %all-to-all-start.6 = ((bf16[128,4,256]{2,1,0:T(4,128)(2,1)}), bf16[128,4,256]{2,1,0:T(4,128)(2,1)S(1)}, u32[]{:S(2)}, u32[]{:S(2)}) async-start(bf16[128,4,256]{2,1,0:T(4,128)(2,1)} %get-tuple-element.738), calls=%async_computation.6 | async-start | bytes 524288 | tf_op jit(solution)/shard_map/all_to_all | solution.py:11
  144.8 73.4 %copy-start.9 = (s32[2048]{0:T(1024)S(1)}, s32[2048]{0:T(1024)}, u32[]{:S(2)}) copy-start(s32[2048]{0:T(1024)} %get-tuple-element.1045) | copy-start | bytes 24580
  212.5 29.4 %all-to-all-start.4 = ((bf16[128,4,256]{2,1,0:T(4,128)(2,1)}), bf16[128,4,256]{2,1,0:T(4,128)(2,1)S(1)}, u32[]{:S(2)}, u32[]{:S(2)}) async-start(bf16[128,4,256]{2,1,0:T(4,128)(2,1)} %get-tuple-element.739), calls=%async_computation.4 | async-start | bytes 524288 | tf_op jit(solution)/shard_map/all_to_all | solution.py:11
  241.9 34.6 %all-to-all-start.7 = ((f32[128,4,256]{2,1,0:T(4,128)}), f32[128,4,256]{2,1,0:T(4,128)S(1)}, u32[]{:S(2)}, u32[]{:S(2)}) async-start(f32[128,4,256]{2,1,0:T(4,128)} %reshape.88), calls=%async_computation.7 | async-start | bytes 1048576 | tf_op jit(solution)/shard_map/all_to_all | solution.py:19
  276.5 11.1 %copy-start.14 = (s32[512]{0:T(512)S(1)}, s32[512]{0:T(512)}, u32[]{:S(2)}) copy-start(s32[512]{0:T(512)} %eq.293) | copy-start | bytes 6148
  276.5 23.4 %all-to-all-start.5 = ((f32[128,4,256]{2,1,0:T(4,128)}), f32[128,4,256]{2,1,0:T(4,128)S(1)}, u32[]{:S(2)}, u32[]{:S(2)}) async-start(f32[128,4,256]{2,1,0:T(4,128)} %reshape.85), calls=%async_computation.5 | async-start | bytes 1048576 | tf_op jit(solution)/shard_map/all_to_all | solution.py:19
  286.3 157.5 %all-reduce.3.cloned.1.call-start = ((), (), s32[]{:S(2)}) async-start(), calls=%async_computation.8 | async-start | bytes 2097152 | tf_op jit(solution)/shard_map/psum | solution.py:120
Sparse Core Ops, SparseCore 0:
  293.1 150.6 all-reduce.2
where the time goes:
time: 455 us; the launch traced here: 453 us
  waiting for transfers between devices  168 us (37%)
  matrix products  88.7 us (19%)
  blocking collectives  67.1 us (15%)
  starting transfers between devices  64.9 us (14%)
  local copies, waits for them, and re-layouts  28.8 us (6%)
  other arithmetic  21.3 us (5%)
  between operations  14.5 us (3%)
    psum x1, waiting for transfers between devices, shards(): lax.psum((early_self, early_nbr, early_bias, late_self, late_nbr), ('dom'...  140 us
    dot_general x20, matrix products, tdot(): lax.dot_general(left, right, (((0,), (0,)), ((), ())), preferred_element_...  72.1 us
    psum x1, blocking collectives, shards(): lax.psum((early_self, early_nbr, early_bias, late_self, late_nbr), ('dom'...  67.1 us
    all_to_all x4, starting transfers between devices, to_masters(): lax.all_to_all(sectioned_rows, ('dom', 'sub'), split_axis=0, concat_axis=...  39.1 us
    all_to_all x4, starting transfers between devices, to_mirrors(): lax.all_to_all(picked_rows, ('dom', 'sub'), split_axis=0, concat_axis=0,...  25.8 us
    all_to_all x4, waiting for transfers between devices, to_masters(): lax.all_to_all(sectioned_rows, ('dom', 'sub'), split_axis=0, concat_axis=...  17.7 us
    lt x16, other arithmetic, one_block(): jnp.arange(block_rows, dtype=jnp.int32) + offset < live_count  10.4 us
    dot_general x4, matrix products, to_masters(): jnp.dot(placing, flat_rows, precision=lax.Precision.HIGHEST, preferred_el...  10.2 us
  transfers between devices with their start and end apart: 9, of which 4 were waited for; matrix products, arithmetic and copies ran while one was open for 25% of the time, Pallas kernels for 0%

commit v1 on v0

--- a/solution.py
+++ b/solution.py
@@ -118,7 +118,7 @@
         dot_transposed(grad_z_one, w_self_one) + gather_sum(message_one, targets, sources)
     ).astype(jnp.bfloat16)
     self_one, nbr_one, bias_sum, self_two, nbr_two = lax.psum(
-        (early_self, early_nbr, early_bias, late_self, late_nbr), ("dom", "sub")
+        lax.psum((early_self, early_nbr, early_bias, late_self, late_nbr), "dom"), "sub"
     )
     norm_factor = jnp.float32(node_dev * lax.axis_size("dom") * lax.axis_size("sub")) ** (-0.5)
     grad_weights = jnp.stack([self_one, nbr_one, self_two, nbr_two]) * norm_factor

time: 455 us -> 376 us (0.83)
  waiting for transfers between devices: 168 us -> 103 us
  blocking collectives: 67.1 us -> 53.4 us
  local copies, waits for them, and re-layouts: 28.8 us -> 34.6 us
  starting transfers between devices: 64.9 us -> 59.8 us
    psum x1 -> x2, waiting for transfers between devices: 140 us -> 65.1 us  [the longest x1 60.7 us: shards(): lax.psum(lax.psum((early_self, early_nbr, early_bias, late_self, late_nbr...]
    psum x1 -> x2, blocking collectives: 67.1 us -> 53.4 us  [the longest x1 34.6 us: shards(): lax.psum((early_self, early_nbr, early_bias, late_self, late_nbr), 'dom')]
    all_to_all x4, waiting for transfers between devices: 9.69 us -> 18.6 us  [to_mirrors(): lax.all_to_all(picked_rows, ('dom', 'sub'), split_axis=0, concat_axis=0,...]
    all_to_all x4, starting transfers between devices: 39.1 us -> 33.9 us  [to_masters(): lax.all_to_all(sectioned_rows, ('dom', 'sub'), split_axis=0, concat_axis=...]
  transfers between devices with their start and end apart: 9 -> 10, of which waited for: 4 -> 6; matrix products, arithmetic and copies ran while one was open for 25% -> 30% of each run, Pallas kernels for 0% -> 0%
where the time goes in v1:
time: 376 us; the launch traced here: 372 us
  waiting for transfers between devices  103 us (27%)
  matrix products  85.7 us (23%)
  starting transfers between devices  59.8 us (16%)
  blocking collectives  53.4 us (14%)
  local copies, waits for them, and re-layouts  34.6 us (9%)
  other arithmetic  21.2 us (6%)
  between operations  14.5 us (4%)
    dot_general x20, matrix products, tdot(): lax.dot_general(left, right, (((0,), (0,)), ((), ())), preferred_element_...  68.9 us
    psum x1, waiting for transfers between devices, shards(): lax.psum(lax.psum((early_self, early_nbr, early_bias, late_self, late_nbr...  60.7 us
    psum x1, blocking collectives, shards(): lax.psum((early_self, early_nbr, early_bias, late_self, late_nbr), 'dom')  34.6 us
    all_to_all x4, starting transfers between devices, to_masters(): lax.all_to_all(sectioned_rows, ('dom', 'sub'), split_axis=0, concat_axis=...  33.9 us
    all_to_all x4, starting transfers between devices, to_mirrors(): lax.all_to_all(picked_rows, ('dom', 'sub'), split_axis=0, concat_axis=0,...  25.6 us
    all_to_all x4, waiting for transfers between devices, to_masters(): lax.all_to_all(sectioned_rows, ('dom', 'sub'), split_axis=0, concat_axis=...  19.1 us
    psum x1, blocking collectives, shards(): lax.psum(lax.psum((early_self, early_nbr, early_bias, late_self, late_nbr...  18.9 us
    all_to_all x4, waiting for transfers between devices, to_mirrors(): lax.all_to_all(picked_rows, ('dom', 'sub'), split_axis=0, concat_axis=0,...  18.6 us
  transfers between devices with their start and end apart: 10, of which 6 were waited for; matrix products, arithmetic and copies ran while one was open for 30% of the time, Pallas kernels for 0%

profile of v1, /device:TPU:1, one launch (start us, length us, event | category | flops | bytes accessed | tf_op | source)
XLA Modules:
  0.0 372.5 jit_solution(5858406626196903632)
XLA Ops:
  9.5 1.2 fusion.75
  10.8 2.0 gather_fusion
  12.9 2.0 gather_fusion.1
  15.0 1.1 broadcast_select_fusion.2
  16.2 11.9 %all-to-all-start = ((bf16[128,4,256]{2,1,0:T(4,128)(2,1)}), bf16[128,4,256]{2,1,0:T(4,128)(2,1)}, u32[]{:S(2)}, u32[]{:S(2)}) async-start(bf16[128,4,256]{2,1,0:T(4,128)(2,1)} %get-tuple-element.745), calls=%async_computation | async-start | bytes 524288 | tf_op jit(solution)/shard_map/all_to_all | solution.py:11
  29.0 9.7 %all-to-all-done = bf16[128,4,256]{2,1,0:T(4,128)(2,1)} async-done(((bf16[128,4,256]{2,1,0:T(4,128)(2,1)}), bf16[128,4,256]{2,1,0:T(4,128)(2,1)}, u32[]{:S(2)}, u32[]{:S(2)}) %all-to-all-start) | async-done | bytes 262176 | tf_op jit(solution)/shard_map/all_to_all | solution.py:11
  38.7 4.6 %all-to-all-start.2 = ((bf16[128,4,256]{2,1,0:T(4,128)(2,1)}), bf16[128,4,256]{2,1,0:T(4,128)(2,1)S(1)}, u32[]{:S(2)}, u32[]{:S(2)}) async-start(bf16[128,4,256]{2,1,0:T(4,128)(2,1)} %get-tuple-element.744), calls=%async_computation.2 | async-start | bytes 524288 | tf_op jit(solution)/shard_map/all_to_all | solution.py:11
  43.3 1.7 reshape.78
  45.0 1.9 pad_maximum_fusion
  46.9 20.3 %while.60 = (s32[]{:T(128)}, f32[1536,256]{1,0:T(8,128)S(1)}, s32[2048]{0:T(1024)S(1)}, s32[2048]{0:T(1024)}, s32[]{:T(128)}, /*index=5*/bf16[1536,256]{1,0:T(8,...) while((s32[]{:T(128)}, f32[1536,256]{1,0:T(8,128)S(1)}, s32[2048]{0:T(1024)S(1)}, ...), condition=%wide.region_1.3_spmd.clone.clone, body=%wide.region_0.0_spmd.clone.clone.sunk | while | flops 808584192 | bytes 3945645 | solution.py:53
  48.4 3.6 fusion.128
  53.5 3.6 fusion.128
  58.6 3.6 fusion.128
  63.7 3.6 fusion.128
  67.3 1.1 reshape.79
  68.6 9.8 %all-to-all-start.1 = ((f32[128,4,256]{2,1,0:T(4,128)}), f32[128,4,256]{2,1,0:T(4,128)S(1)}, u32[]{:S(2)}, u32[]{:S(2)}) async-start(f32[128,4,256]{2,1,0:T(4,128)} %reshape.79), calls=%async_computation.1 | async-start | bytes 1048576 | tf_op jit(solution)/shard_map/all_to_all | solution.py:19
  78.5 22.7 %while.61 = (s32[]{:T(128)}, f32[1536,256]{1,0:T(8,128)}, s32[2048]{0:T(1024)}, s32[2048]{0:T(1024)S(1)}, s32[]{:T(128)}, /*index=5*/bf16[1536,256]{1,0:T(8,128)...) while((s32[]{:T(128)}, f32[1536,256]{1,0:T(8,128)}, s32[2048]{0:T(1024)}, ...), condition=%wide.region_3.5_spmd.clone.clone, body=%wide.region_2.4_spmd.clone.clone.sunk | while | flops 808584192 | bytes 3945645 | solution.py:53
  80.0 3.1 fusion.131
  84.6 4.5 %fusion.131 = f32[1536,256]{1,0:T(8,128)} fusion(f32[1536,256]{1,0:T(8,128)} %get-tuple-element.909, s32[512]{0:T(512)S(1)} %dynamic_slice.82, bf16[1536,256]{1,0:T(8,128)(2,1)S(1)} %get-tuple-element.923, s32[512]{0:T(512)S(1)} %dynamic_slice.83, pred[512]{0:T(512)(128)(4,1)S(1)} %add_compare_fusion.9, pred[]{:T(512)S(6)} %compare.13), kind=kOutput, calls=%fused_computation.24.clone.1 | convolution fusion | flops 808583168 | bytes 3936769 | tf_op jit(solution)/shard_map/while/body/eval_jaxpr/dot_general | solution.py:57
  90.7 4.5 %fusion.131 = f32[1536,256]{1,0:T(8,128)} fusion(f32[1536,256]{1,0:T(8,128)} %get-tuple-element.909, s32[512]{0:T(512)S(1)} %dynamic_slice.82, bf16[1536,256]{1,0:T(8,128)(2,1)S(1)} %get-tuple-element.923, s32[512]{0:T(512)S(1)} %dynamic_slice.83, pred[512]{0:T(512)(128)(4,1)S(1)} %add_compare_fusion.9, pred[]{:T(512)S(6)} %compare.13), kind=kOutput, calls=%fused_computation.24.clone.1 | convolution fusion | flops 808583168 | bytes 3936769 | tf_op jit(solution)/shard_map/while/body/eval_jaxpr/dot_general | solution.py:57
  96.7 4.5 %fusion.131 = f32[1536,256]{1,0:T(8,128)} fusion(f32[1536,256]{1,0:T(8,128)} %get-tuple-element.909, s32[512]{0:T(512)S(1)} %dynamic_slice.82, bf16[1536,256]{1,0:T(8,128)(2,1)S(1)} %get-tuple-element.923, s32[512]{0:T(512)S(1)} %dynamic_slice.83, pred[512]{0:T(512)(128)(4,1)S(1)} %add_compare_fusion.9, pred[]{:T(512)S(6)} %compare.13), kind=kOutput, calls=%fused_computation.24.clone.1 | convolution fusion | flops 808583168 | bytes 3936769 | tf_op jit(solution)/shard_map/while/body/eval_jaxpr/dot_general | solution.py:57
  101.2 1.1 slice.27
  103.3 9.8 %all-to-all-start.3 = ((f32[128,4,256]{2,1,0:T(4,128)}), f32[128,4,256]{2,1,0:T(4,128)S(1)}, u32[]{:S(2)}, u32[]{:S(2)}) async-start(f32[128,4,256]{2,1,0:T(4,128)} %reshape.82), calls=%async_computation.3 | async-start | bytes 1048576 | tf_op jit(solution)/shard_map/all_to_all | solution.py:19
  113.1 1.3 fusion.82
  114.5 3.3 fusion.66
  117.8 8.8 %all-to-all-done.3 = f32[128,4,256]{2,1,0:T(4,128)S(1)} async-done(((f32[128,4,256]{2,1,0:T(4,128)}), f32[128,4,256]{2,1,0:T(4,128)S(1)}, u32[]{:S(2)}, u32[]{:S(2)}) %all-to-all-start.3) | async-done | bytes 524320 | tf_op jit(solution)/shard_map/all_to_all | solution.py:19
  126.7 1.0 reshape.83
  127.6 2.5 fusion.73
  130.2 1.3 multiply_convert_fusion
  131.6 1.1 convert_reduce_fusion
  133.0 2.0 gather_fusion.2
  135.1 2.0 gather_fusion.3
  137.1 1.8 broadcast_select_fusion
  138.9 4.6 %all-to-all-start.6 = ((bf16[128,4,256]{2,1,0:T(4,128)(2,1)}), bf16[128,4,256]{2,1,0:T(4,128)(2,1)S(1)}, u32[]{:S(2)}, u32[]{:S(2)}) async-start(bf16[128,4,256]{2,1,0:T(4,128)(2,1)} %get-tuple-element.742), calls=%async_computation.6 | async-start | bytes 524288 | tf_op jit(solution)/shard_map/all_to_all | solution.py:11
  143.6 2.1 fusion.83
  145.7 8.9 %all-to-all-done.6 = bf16[128,4,256]{2,1,0:T(4,128)(2,1)S(1)} async-done(((bf16[128,4,256]{2,1,0:T(4,128)(2,1)}), bf16[128,4,256]{2,1,0:T(4,128)(2,1)S(1)}, u32[]{:S(2)}, u32[]{:S(2)}) %all-to-all-start.6) | async-done | bytes 262176 | tf_op jit(solution)/shard_map/all_to_all | solution.py:11
  154.6 4.5 %all-to-all-start.4 = ((bf16[128,4,256]{2,1,0:T(4,128)(2,1)}), bf16[128,4,256]{2,1,0:T(4,128)(2,1)S(1)}, u32[]{:S(2)}, u32[]{:S(2)}) async-start(bf16[128,4,256]{2,1,0:T(4,128)(2,1)} %get-tuple-element.743), calls=%async_computation.4 | async-start | bytes 524288 | tf_op jit(solution)/shard_map/all_to_all | solution.py:11
  160.1 24.4 %while.63 = (s32[]{:T(128)}, f32[1536,256]{1,0:T(8,128)}, s32[2048]{0:T(1024)}, s32[2048]{0:T(1024)S(1)}, s32[]{:T(128)}, /*index=5*/bf16[1536,256]{1,0:T(8,128)(2,1)}, s32[]{:T(128)}, s32[]{:T(128)}, s32[]{:T(128)}, s32[]{:T(128)}) while((s32[]{:T(128)}, f32[1536,256]{1,0:T(8,128)}, s32[2048]{0:T(1024)}, ...), condition=%wide.region_13.15_spmd.clone.clone, body=%wide.region_12.14_spmd.clone.clone.sunk | while | flops 808584192 | bytes 3945645 | solution.py:53
  161.6 4.2 %fusion.137 = f32[1536,256]{1,0:T(8,128)} fusion(f32[1536,256]{1,0:T(8,128)} %get-tuple-element.999, s32[512]{0:T(512)S(1)} %dynamic_slice.86, bf16[1536,256]{1,0:T(8,128)(2,1)} %get-tuple-element.1013, s32[512]{0:T(512)S(1)} %dynamic_slice.87, pred[512]{0:T(512)(128)(4,1)S(1)} %add_compare_fusion.11, pred[]{:T(512)S(6)} %compare.15), kind=kOutput, calls=%fused_computation.46.clone.1 | convolution fusion | flops 808583168 | bytes 3936769 | tf_op jit(solution)/shard_map/while/body/eval_jaxpr/dot_general | solution.py:57
  167.3 4.7 %fusion.137 = f32[1536,256]{1,0:T(8,128)} fusion(f32[1536,256]{1,0:T(8,128)} %get-tuple-element.999, s32[512]{0:T(512)S(1)} %dynamic_slice.86, bf16[1536,256]{1,0:T(8,128)(2,1)} %get-tuple-element.1013, s32[512]{0:T(512)S(1)} %dynamic_slice.87, pred[512]{0:T(512)(128)(4,1)S(1)} %add_compare_fusion.11, pred[]{:T(512)S(6)} %compare.15), kind=kOutput, calls=%fused_computation.46.clone.1 | convolution fusion | flops 808583168 | bytes 3936769 | tf_op jit(solution)/shard_map/while/body/eval_jaxpr/dot_general | solution.py:57
  173.5 4.7 %fusion.137 = f32[1536,256]{1,0:T(8,128)} fusion(f32[1536,256]{1,0:T(8,128)} %get-tuple-element.999, s32[512]{0:T(512)S(1)} %dynamic_slice.86, bf16[1536,256]{1,0:T(8,128)(2,1)} %get-tuple-element.1013, s32[512]{0:T(512)S(1)} %dynamic_slice.87, pred[512]{0:T(512)(128)(4,1)S(1)} %add_compare_fusion.11, pred[]{:T(512)S(6)} %compare.15), kind=kOutput, calls=%fused_computation.46.clone.1 | convolution fusion | flops 808583168 | bytes 3936769 | tf_op jit(solution)/shard_map/while/body/eval_jaxpr/dot_general | solution.py:57
  179.8 4.7 %fusion.137 = f32[1536,256]{1,0:T(8,128)} fusion(f32[1536,256]{1,0:T(8,128)} %get-tuple-element.999, s32[512]{0:T(512)S(1)} %dynamic_slice.86, bf16[1536,256]{1,0:T(8,128)(2,1)} %get-tuple-element.1013, s32[512]{0:T(512)S(1)} %dynamic_slice.87, pred[512]{0:T(512)(128)(4,1)S(1)} %add_compare_fusion.11, pred[]{:T(512)S(6)} %compare.15), kind=kOutput, calls=%fused_computation.46.clone.1 | convolution fusion | flops 808583168 | bytes 3936769 | tf_op jit(solution)/shard_map/while/body/eval_jaxpr/dot_general | solution.py:57
  184.5 1.1 slice.31
  186.5 9.8 %all-to-all-start.7 = ((f32[128,4,256]{2,1,0:T(4,128)}), f32[128,4,256]{2,1,0:T(4,128)S(1)}, u32[]{:S(2)}, u32[]{:S(2)}) async-start(f32[128,4,256]{2,1,0:T(4,128)} %reshape.88), calls=%async_computation.7 | async-start | bytes 1048576 | tf_op jit(solution)/shard_map/all_to_all | solution.py:19
  196.6 1.0 convolution_bitcast_fusion
  197.6 1.1 fusion.84
  199.7 10.2 %all-to-all-done.7 = f32[128,4,256]{2,1,0:T(4,128)S(1)} async-done(((f32[128,4,256]{2,1,0:T(4,128)}), f32[128,4,256]{2,1,0:T(4,128)S(1)}, u32[]{:S(2)}, u32[]{:S(2)}) %all-to-all-start.7) | async-done | bytes 524320 | tf_op jit(solution)/shard_map/all_to_all | solution.py:19
  210.1 2.3 fusion.72
  212.4 1.1 fusion.85
  213.9 20.4 %while.62 = (s32[]{:T(128)}, f32[1536,256]{1,0:T(8,128)S(1)}, s32[2048]{0:T(1024)S(1)}, s32[2048]{0:T(1024)}, s32[]{:T(128)}, /*index=5*/bf16[1536,256]{1,0:T(8,...) while((s32[]{:T(128)}, f32[1536,256]{1,0:T(8,128)S(1)}, s32[2048]{0:T(1024)S(1)}, ...), condition=%wide.region_5.7_spmd.clone.clone, body=%wide.region_4.6_spmd.clone.clone.sunk | while | flops 808584192 | bytes 3945645 | solution.py:53
  215.4 3.6 fusion.134
  220.5 3.6 fusion.134
  225.6 3.6 fusion.134
  230.7 3.6 fusion.134
  234.4 1.1 reshape.85
  235.6 4.6 %all-to-all-start.5 = ((f32[128,4,256]{2,1,0:T(4,128)}), f32[128,4,256]{2,1,0:T(4,128)S(1)}, u32[]{:S(2)}, u32[]{:S(2)}) async-start(f32[128,4,256]{2,1,0:T(4,128)} %reshape.85), calls=%async_computation.5 | async-start | bytes 1048576 | tf_op jit(solution)/shard_map/all_to_all | solution.py:19
  240.3 34.6 %psum.78 = f32[256]{0:T(256)S(1)} all-reduce(f32[256]{0:T(256)S(1)} %copy-done.16), channel_id=1, replica_groups=mesh['dom'=16,'sub'=8] {'dom'}, use_global_device_ids=true, to_apply=%region_17.19 | all-reduce | flops 256 | bytes 2048 | tf_op jit(solution)/shard_map/psum | solution.py:121
  274.8 18.9 %psum.79 = f32[256]{0:T(256)S(1)} all-reduce(f32[256]{0:T(256)S(1)} %psum.78), channel_id=1, replica_groups=mesh['dom'=16,'sub'=8] {'sub'}, use_global_device_ids=true, to_apply=%region_18.20 | all-reduce | flops 256 | bytes 2048 | tf_op jit(solution)/shard_map/psum | solution.py:120
  294.5 4.4 %all-reduce.5.cloned.1.call-done = (f32[256,256]{0,1:T(8,128)}, f32[256,256]{0,1:T(8,128)}, f32[256,256]{0,1:T(8,128)}, f32[256,256]{0,1:T(8,128)}) async-done(((f32[256,256]{0,1:T(8,128)}, f32[256,256]{0,1:T(8,128)}, f32[256,256]{0,1:T(8,128)}, f32[256,256]{0,1:T(8,128)}), (f32[256,256]{0,1:T(8,128)}, f32[256,256]{0,1:T(8,128)}, f32[256,256]{0,1:T(8,128)}, ...) | async-done | bytes 1048592 | tf_op jit(solution)/shard_map/psum | solution.py:121
  298.9 2.3 fusion.69
  301.2 1.1 fusion.76
  302.3 60.7 %all-reduce.7.cloned.1.call-done = (f32[1,256,256]{1,2,0:T(8,128)}, f32[1,256,256]{1,2,0:T(8,128)}, f32[1,256,256]{1,2,0:T(8,128)}, f32[1,256,256]{1,2,0:T(8,128)}) async-done(((f32[1,256,256]{1,2,0:T(8,128)}, f32[1,256,256]{1,2,0:T(8,128)}, f32[1,256,256]{1,2,0:T(8,128)}, f32[1,256,256]{1,2,0:T(8,128)}), (f32[1,256,256]{1,2,0:T(8,128)}, f32[1,256,256]{1,2,0:T(8,128)}, f32[1,256,256]{1,2,0:T(8,128)}, ...) | async-done | bytes 1048592 | tf_op jit(solution)/shard_map/psum | solution.py:120
  363.0 1.3 maximum_multiply_fusion
  364.4 1.3 copy.35
  (124 shorter events, 34.1 us)
Async XLA Ops:
  7.2 2.4 copy-start
  10.8 2.0 copy-start.1
  14.8 13.3 %copy-start.12 = (s32[1,128,4]{1,2,0:T(4,128)S(1)}, s32[1,128,4]{1,2,0:T(4,128)}, u32[]{:S(2)}) copy-start(s32[1,128,4]{1,2,0:T(4,128)} %param.30) | copy-start | bytes 6148
  15.0 1.2 copy-start.10
  16.2 30.7 %copy-start.9 = (s32[1,2048]{1,0:T(1,128)S(1)}, s32[1,2048]{1,0:T(1,128)}, u32[]{:S(2)}) copy-start(s32[1,2048]{1,0:T(1,128)} %param.31) | copy-start | bytes 24580
  16.2 22.5 %all-to-all-start = ((bf16[128,4,256]{2,1,0:T(4,128)(2,1)}), bf16[128,4,256]{2,1,0:T(4,128)(2,1)}, u32[]{:S(2)}, u32[]{:S(2)}) async-start(bf16[128,4,256]{2,1,0:T(4,128)(2,1)} %get-tuple-element.745), calls=%async_computation | async-start | bytes 524288 | tf_op jit(solution)/shard_map/all_to_all | solution.py:11
  38.7 29.8 %all-to-all-start.2 = ((bf16[128,4,256]{2,1,0:T(4,128)(2,1)}), bf16[128,4,256]{2,1,0:T(4,128)(2,1)S(1)}, u32[]{:S(2)}, u32[]{:S(2)}) async-start(bf16[128,4,256]{2,1,0:T(4,128)(2,1)} %get-tuple-element.744), calls=%async_computation.2 | async-start | bytes 524288 | tf_op jit(solution)/shard_map/all_to_all | solution.py:11
  67.2 1.4 copy-start.4
  68.6 34.7 %all-to-all-start.1 = ((f32[128,4,256]{2,1,0:T(4,128)}), f32[128,4,256]{2,1,0:T(4,128)S(1)}, u32[]{:S(2)}, u32[]{:S(2)}) async-start(f32[128,4,256]{2,1,0:T(4,128)} %reshape.79), calls=%async_computation.1 | async-start | bytes 1048576 | tf_op jit(solution)/shard_map/all_to_all | solution.py:19
  101.2 11.8 %copy-start.8 = (bf16[256,256]{1,0:T(8,128)(2,1)S(1)}, bf16[256,256]{1,0:T(8,128)(2,1)}, u32[]{:S(2)}) copy-start(bf16[256,256]{1,0:T(8,128)(2,1)} %param.24) | copy-start | bytes 393220
  103.3 23.4 %all-to-all-start.3 = ((f32[128,4,256]{2,1,0:T(4,128)}), f32[128,4,256]{2,1,0:T(4,128)S(1)}, u32[]{:S(2)}, u32[]{:S(2)}) async-start(f32[128,4,256]{2,1,0:T(4,128)} %reshape.82), calls=%async_computation.3 | async-start | bytes 1048576 | tf_op jit(solution)/shard_map/all_to_all | solution.py:19
  113.1 1.5 copy-start.13
  117.8 12.3 %copy-start.6 = (f32[1024,256]{1,0:T(8,128)S(1)}, f32[1024,256]{1,0:T(8,128)}, u32[]{:S(2)}) copy-start(f32[1024,256]{1,0:T(8,128)} %fusion.82) | copy-start | bytes 3145732
  117.8 12.3 %copy-start.11 = (bf16[256,256]{1,0:T(8,128)(2,1)S(1)}, bf16[256,256]{1,0:T(8,128)(2,1)}, u32[]{:S(2)}) copy-start(bf16[256,256]{1,0:T(8,128)(2,1)} %param.25) | copy-start | bytes 393220
  130.1 1.3 copy-start.7
  130.1 1.4 copy-start.5
  130.2 1.4 copy-start.17
  138.9 15.6 %all-to-all-start.6 = ((bf16[128,4,256]{2,1,0:T(4,128)(2,1)}), bf16[128,4,256]{2,1,0:T(4,128)(2,1)S(1)}, u32[]{:S(2)}, u32[]{:S(2)}) async-start(bf16[128,4,256]{2,1,0:T(4,128)(2,1)} %get-tuple-element.742), calls=%async_computation.6 | async-start | bytes 524288 | tf_op jit(solution)/shard_map/all_to_all | solution.py:11
  154.6 31.9 %all-to-all-start.4 = ((bf16[128,4,256]{2,1,0:T(4,128)(2,1)}), bf16[128,4,256]{2,1,0:T(4,128)(2,1)S(1)}, u32[]{:S(2)}, u32[]{:S(2)}) async-start(bf16[128,4,256]{2,1,0:T(4,128)(2,1)} %get-tuple-element.743), calls=%async_computation.4 | async-start | bytes 524288 | tf_op jit(solution)/shard_map/all_to_all | solution.py:11
  186.5 23.4 %all-to-all-start.7 = ((f32[128,4,256]{2,1,0:T(4,128)}), f32[128,4,256]{2,1,0:T(4,128)S(1)}, u32[]{:S(2)}, u32[]{:S(2)}) async-start(f32[128,4,256]{2,1,0:T(4,128)} %reshape.88), calls=%async_computation.7 | async-start | bytes 1048576 | tf_op jit(solution)/shard_map/all_to_all | solution.py:19
  196.3 102.6 %all-reduce.5.cloned.1.call-start = ((), (), s32[]{:S(2)}) async-start(), calls=%async_computation.8 | async-start | bytes 2097152 | tf_op jit(solution)/shard_map/psum | solution.py:121
  198.6 11.4 %copy-start.14 = (s32[512]{0:T(512)S(1)}, s32[512]{0:T(512)}, u32[]{:S(2)}) copy-start(s32[512]{0:T(512)} %eq.293) | copy-start | bytes 6148
  212.4 1.5 copy-start.2
  234.3 1.3 copy-start.3
  234.3 6.0 %copy-start.16 = (f32[256]{0:T(256)S(1)}, f32[256]{0:T(256)}, u32[]{:S(2)}) copy-start(f32[256]{0:T(256)} %get-tuple-element.748) | copy-start | bytes 3076
  235.4 63.4 %copy-start.15 = (s32[512]{0:T(512)S(1)}, s32[512]{0:T(512)}, u32[]{:S(2)}) copy-start(s32[512]{0:T(512)} %eq.293) | copy-start | bytes 6148
  235.6 58.7 %all-to-all-start.5 = ((f32[128,4,256]{2,1,0:T(4,128)}), f32[128,4,256]{2,1,0:T(4,128)S(1)}, u32[]{:S(2)}, u32[]{:S(2)}) async-start(f32[128,4,256]{2,1,0:T(4,128)} %reshape.85), calls=%async_computation.5 | async-start | bytes 1048576 | tf_op jit(solution)/shard_map/all_to_all | solution.py:19
  240.2 122.8 %all-reduce.7.cloned.1.call-start = ((), (), s32[]{:S(2)}) async-start(), calls=%async_computation.9 | async-start | bytes 2097152 | tf_op jit(solution)/shard_map/psum | solution.py:120
Sparse Core Ops, SparseCore 0:
  213.6 85.1 all-reduce.4
  301.4 61.6 all-reduce.6
